TPU v7x, 256 devices: a whole 4x4x8 slice. The times are simulated.
256 devices in a mesh: expert: 64 (over z, y, core), replica: 4 (over x).
Axes of the slice: x: 4, y: 4, z: 8, core: 2. Of those that a mesh axis runs over, the one named last changes fastest.
Arguments:
- hidden_first: bfloat16 [2048, 4096], P(('expert', 'replica')), may hold values from -40 to 40
- hidden_second: bfloat16 [2048, 4096], P(('expert', 'replica')), may hold values from -40 to 40
- routes_first: int32 [2048, 8], P(('expert', 'replica')), may hold values from 0 to 63, all different within a row; in each aligned block of 8 rows (0 to 7, 8 to 15, ...) at most 2 rows name the same one
- routes_second: int32 [2048, 8], P(('expert', 'replica')), may hold values from 0 to 63, all different within a row; in each aligned block of 8 rows (0 to 7, 8 to 15, ...) at most 2 rows name the same one
- mixing_first: float32 [2048, 8], P(('expert', 'replica')), may hold values from 0.05 to 0.5
- mixing_second: float32 [2048, 8], P(('expert', 'replica')), may hold values from 0.05 to 0.5
- norm_gain: float32 [4096], replicated, may hold values from 0.1 to 1.9
- expert_owner: int32 [64], replicated, may hold values from 0 to 63, each once
- swap_flags: int32 [64], replicated, may hold values from 0 to 1, as said below
- gate_up_values: bfloat16 [64, 2, 4096, 1024], P('expert', None, None, 'replica'), may hold values from -0.09375 to 0.09375
- gate_up_scales: bfloat16 [64, 2, 32, 8], P('expert', None, None, 'replica'), may hold values from 0.5 to 2
- down_values: bfloat16 [64, 1024, 4096], P('expert', 'replica'), may hold values from -0.1875 to 0.1875
- down_scales: bfloat16 [64, 8, 32], P('expert', 'replica'), may hold values from 0.5 to 2
Outputs:
- output_first: bfloat16 [2048, 4096], P(('expert', 'replica'))
- output_second: bfloat16 [2048, 4096], P(('expert', 'replica'))
- gate_up_moved: bfloat16 [64, 2, 4096, 1024], P('expert', None, None, 'replica')
- gate_up_scales_moved: bfloat16 [64, 2, 32, 8], P('expert', None, None, 'replica')
- down_moved: bfloat16 [64, 1024, 4096], P('expert', 'replica')
- down_scales_moved: bfloat16 [64, 8, 32], P('expert', 'replica')
Inputs may be any that keep to these rules, and one draw needn't show every extreme that they name: swap_flags[d] equals swap_flags[(d + 32) mod 64].
All inputs are finite; a program needn't handle non-finite values.
Results may differ from a plain program's by a relative error of at most 0.012.
Values may be sent and summed in bfloat16 or wider, within the bound.
No kernel may reach another device: no remote copies, remote signals or barrier semaphores. Data moves between devices by JAX's collectives and lax.ppermute only.
A program may use at most 128 MiB of HBM per device.

v0:
```python
import jax
import jax.numpy as jnp
from jax import lax
from jax.sharding import PartitionSpec as P


def partner(block, axis, bit):
    count = lax.axis_size(axis)
    route = []
    for low in range(count):
        high = low | 1 << bit
        if high != low and high < count:
            route += [(low, high), (high, low)]
    return lax.ppermute(block, axis, route)


def dequantize(values, scales):
    height, breadth = (values.shape[-2], values.shape[-1])
    block_rows, block_cols = (scales.shape[-2], scales.shape[-1])
    leading = values.shape[:-2]
    blocked = values.astype(jnp.float32).reshape(
        leading + (block_rows, height // block_rows, block_cols, breadth // block_cols)
    )
    scaled = blocked * scales.astype(jnp.float32)[..., :, None, :, None]
    return scaled.reshape(values.shape).astype(jnp.bfloat16)


def rms_normed(hidden, norm_gain):
    widened = hidden.astype(jnp.float32)
    inverse_rms = lax.rsqrt(jnp.mean(widened * widened, axis=-1, keepdims=True) + 1e-06)
    return (widened * inverse_rms * norm_gain).astype(jnp.bfloat16)


def rounded(partial_sum):
    return lax.optimization_barrier(partial_sum.astype(jnp.bfloat16)).astype(jnp.float32)


def expert_partial(token_rows, weights):
    gate_up, down_proj = weights
    gate_act = jnp.dot(token_rows, gate_up[0], preferred_element_type=jnp.float32)
    up_act = jnp.dot(token_rows, gate_up[1], preferred_element_type=jnp.float32)
    inner_act = (jax.nn.silu(gate_act) * up_act).astype(jnp.bfloat16)
    return rounded(jnp.dot(inner_act, down_proj, preferred_element_type=jnp.float32))


def pick_slots(routes, owner_slots, experts, capacity):
    tokens_here, top_count = routes.shape
    expert_ids = jnp.arange(owner_slots.shape[0], dtype=jnp.int32)
    target = jnp.sum(jnp.where(routes[:, :, None] == expert_ids, owner_slots, 0), axis=-1).reshape(
        -1
    )
    device_ids = jnp.arange(experts, dtype=jnp.int32)
    target_hot = (target[:, None] == device_ids).astype(jnp.int32)
    earlier = jnp.cumsum(target_hot, axis=0) - target_hot
    rank_in = jnp.sum(earlier * target_hot, axis=1)
    slot_ids = target * capacity + rank_in
    columns = jnp.arange(experts * capacity, dtype=jnp.int32)
    return (
        (slot_ids[:, None] == columns)
        .astype(jnp.float32)
        .reshape(tokens_here, top_count, experts * capacity)
    )


def finish(partial_terms):
    summed = lax.psum_scatter(
        partial_terms.astype(jnp.bfloat16), "replica", scatter_dimension=0, tiled=True
    )
    return lax.all_to_all(summed, "expert", split_axis=1, concat_axis=1, tiled=True)


def decode_step(hidden, routes, mixing, norm_gain, owner_slots, weights):
    experts = lax.axis_size("expert")
    copies = lax.axis_size("replica")
    tokens_here, top_count = routes.shape
    features = hidden.shape[1]
    capacity = min(tokens_here, max(2, 2 * tokens_here * top_count // experts))
    normed = rms_normed(hidden, norm_gain)
    own_picks = pick_slots(routes, owner_slots, experts, capacity)
    pooled, pooled_routes = (
        lax.all_gather(normed, "replica", axis=0, tiled=True),
        lax.all_gather(routes, "replica", axis=0, tiled=True),
    )
    grouped = pooled_routes.reshape(copies, tokens_here, top_count)
    pick_table = jax.vmap(
        lambda route_group: pick_slots(route_group, owner_slots, experts, capacity)
    )(grouped)
    placing = jnp.sum(pick_table, axis=2).astype(jnp.bfloat16)
    outgoing = jnp.einsum(
        "rts,rtd->rsd",
        placing,
        pooled.reshape(copies, tokens_here, features),
        preferred_element_type=jnp.float32,
    )
    outgoing = outgoing.astype(jnp.bfloat16).reshape(copies, experts, capacity, features)
    arrived = lax.all_to_all(outgoing, "expert", split_axis=1, concat_axis=1, tiled=True)
    slot_count = arrived.shape[2]
    flat_rows = arrived.reshape(-1, features)
    partial_terms = expert_partial(flat_rows, weights).reshape(
        copies, experts, slot_count, features
    )
    returned = finish(partial_terms)
    mixing_matrix = jnp.einsum("tks,tk->ts", own_picks, mixing, precision=lax.Precision.HIGHEST)
    merged = jnp.dot(
        mixing_matrix,
        returned.reshape(experts * capacity, features).astype(jnp.float32),
        precision=lax.Precision.HIGHEST,
    )
    return merged.astype(jnp.bfloat16)


def body(
    hidden_first,
    hidden_second,
    routes_first,
    routes_second,
    mixing_first,
    mixing_second,
    norm_gain,
    expert_owner,
    swap_flags,
    gate_up_values,
    gate_up_scales,
    down_values,
    down_scales,
):
    experts = lax.axis_size("expert")
    halfway = experts // 2
    my_slot = lax.axis_index("expert")
    current = (gate_up_values, gate_up_scales, down_values, down_scales)
    incoming = partner(
        (gate_up_values, gate_up_scales, down_values, down_scales),
        "expert",
        experts.bit_length() - 2,
    )
    slot_ids = jnp.arange(experts, dtype=jnp.int32)
    flagged = jnp.sum(jnp.where(slot_ids == my_slot, swap_flags, 0)) == 1
    moved_arrays = tuple(
        (
            jnp.where(flagged, fresh_piece, stale_piece)
            for fresh_piece, stale_piece in zip(incoming, current)
        )
    )
    weights_before = (
        dequantize(gate_up_values[0], gate_up_scales[0]),
        dequantize(down_values[0], down_scales[0]),
    )
    output_first = decode_step(
        hidden_first, routes_first, mixing_first, norm_gain, expert_owner, weights_before
    )
    owner_flags = jnp.sum(jnp.where(expert_owner[:, None] == slot_ids, swap_flags, 0), axis=1)
    owner_after = jnp.where(owner_flags == 1, (expert_owner + halfway) % experts, expert_owner)
    weights_after = (
        dequantize(moved_arrays[0][0], moved_arrays[1][0]),
        dequantize(moved_arrays[2][0], moved_arrays[3][0]),
    )
    output_second = decode_step(
        hidden_second, routes_second, mixing_second, norm_gain, owner_after, weights_after
    )
    return (
        output_first,
        output_second,
        moved_arrays[0],
        moved_arrays[1],
        moved_arrays[2],
        moved_arrays[3],
    )


def solution(mesh):
    return jax.shard_map(
        body,
        mesh=mesh,
        in_specs=(
            P(("expert", "replica"), None),
            P(("expert", "replica"), None),
            P(("expert", "replica"), None),
            P(("expert", "replica"), None),
            P(("expert", "replica"), None),
            P(("expert", "replica"), None),
            P(),
            P(),
            P(),
            P("expert", None, None, "replica"),
            P("expert", None, None, "replica"),
            P("expert", "replica", None),
            P("expert", "replica", None),
        ),
        out_specs=(
            P(("expert", "replica"), None),
            P(("expert", "replica"), None),
            P("expert", None, None, "replica"),
            P("expert", None, None, "replica"),
            P("expert", "replica", None),
            P("expert", "replica", None),
        ),
        check_vma=False,
    )
```

profile of v0, /device:TPU:1, one launch (start us, length us, event | category | flops | bytes accessed | tf_op | source)
XLA Modules:
  0.0 738.2 jit_solution(4624766096503249148)
XLA Ops:
  8.7 10.4 %all_gather.14 = s32[32,8]{1,0:T(8,128)S(1)} all-gather(s32[8,8]{1,0:T(8,128)} %param.16), channel_id=1, replica_groups=mesh['expert'=64,'replica'=4] {'replica'}, dimensions={0}, use_global_device_ids=true | all-gather | bytes 1280 | tf_op jit(solution)/shard_map/all_gather | solution.py:82
  23.6 9.4 %all_gather.15 = bf16[32,4096]{1,0:T(8,128)(2,1)S(1)} all-gather(bf16[8,4096]{1,0:T(8,128)(2,1)S(1)} %get-tuple-element.13), channel_id=1, replica_groups=mesh['expert'=64,'replica'=4] {'replica'}, dimensions={0}, use_global_device_ids=true | all-gather | bytes 327680 | tf_op jit(solution)/shard_map/all_gather | solution.py:81
  36.3 7.6 %reshape.189 = bf16[4,64,2,4096]{3,2,1,0:T(2,128)(2,1)} reshape(bf16[4,128,4096]{2,1,0:T(8,128)(2,1)} %convolution_convert_fusion.1) | data formatting | bytes 8388608 | tf_op jit(solution)/shard_map/reshape | solution.py:95
  43.9 10.2 %copy.44 = bf16[4,64,2,4096]{3,2,0,1:T(2,128)(2,1)} copy(bf16[4,64,2,4096]{3,2,1,0:T(2,128)(2,1)} %reshape.189) | data formatting | bytes 8388608 | tf_op jit(solution)/shard_map/reshape | solution.py:95
  54.1 18.4 %all-to-all-start.2 = ((bf16[4,64,2,4096]{3,2,0,1:T(2,128)(2,1)}), bf16[4,64,2,4096]{3,2,0,1:T(2,128)(2,1)}, u32[]{:S(2)}, u32[]{:S(2)}) async-start(bf16[4,64,2,4096]{3,2,0,1:T(2,128)(2,1)} %copy.44), calls=%async_computation.3 | async-start | bytes 8388608 | tf_op jit(solution)/shard_map/all_to_all | solution.py:96
  83.5 10.1 %all_gather.12 = s32[32,8]{1,0:T(8,128)S(1)} all-gather(s32[8,8]{1,0:T(8,128)S(1)} %copy-done.4), channel_id=1, replica_groups=mesh['expert'=64,'replica'=4] {'replica'}, dimensions={0}, use_global_device_ids=true | all-gather | bytes 1280 | tf_op jit(solution)/shard_map/all_gather | solution.py:82
  94.9 10.6 %all_gather.13 = bf16[32,4096]{1,0:T(8,128)(2,1)S(1)} all-gather(bf16[8,4096]{1,0:T(8,128)(2,1)S(1)} %get-tuple-element.14), channel_id=1, replica_groups=mesh['expert'=64,'replica'=4] {'replica'}, dimensions={0}, use_global_device_ids=true | all-gather | bytes 327680 | tf_op jit(solution)/shard_map/all_gather | solution.py:81
  108.9 7.8 %reshape.185 = bf16[4,64,2,4096]{3,2,1,0:T(2,128)(2,1)} reshape(bf16[4,128,4096]{2,1,0:T(8,128)(2,1)} %convolution_convert_fusion.3) | data formatting | bytes 8388608 | tf_op jit(solution)/shard_map/reshape | solution.py:95
  116.8 10.2 %copy.39 = bf16[4,64,2,4096]{3,2,0,1:T(2,128)(2,1)} copy(bf16[4,64,2,4096]{3,2,1,0:T(2,128)(2,1)} %reshape.185) | data formatting | bytes 8388608 | tf_op jit(solution)/shard_map/reshape | solution.py:95
  128.2 243.6 %collective-permute-done.3 = bf16[1,2,32]{2,1,0:T(2,128)(2,1)S(1)} collective-permute-done((bf16[1,2,32]{2,1,0:T(2,128)(2,1)S(1)}, bf16[1,2,32]{2,1,0:T(2,128)(2,1)S(1)}, u32[]{:S(2)}, u32[]{:S(2)}) %collective-permute-start.3) | collective-permute-done | bytes 160 | tf_op jit(solution)/shard_map/ppermute | solution.py:14
  378.5 11.5 %mul.143 = f32[2,4096,256]{2,1,0:T(8,128)} reshape(f32[2,32,128,2,128]{4,3,2,1,0:T(2,128)} %mul.142) | data formatting | bytes 16777216 | tf_op jit(solution)/shard_map/mul | solution.py:24
  395.5 11.5 %mul.159 = f32[2,4096,256]{2,1,0:T(8,128)} reshape(f32[2,32,128,2,128]{4,3,2,1,0:T(2,128)} %mul.158) | data formatting | bytes 16777216 | tf_op jit(solution)/shard_map/mul | solution.py:24
  409.9 10.6 %fusion = (bf16[2,4096,256]{2,1,0:T(8,128)(2,1)}, bf16[1,2,4096,256]{3,2,1,0:T(8,128)(2,1)}, bf16[2,4096,256]{2,1,0:T(8,128)(2,1)}) fusion(f32[2,4096,256]{2,1,0:T(8,128)} %mul.159, bf16[1,2,4096,256]{3,2,1,0:T(8,128)(2,1)} %collective-permute-done, bf16[1,2,4096,256]{3,2,1,0:T(8,128)(2,1)S(1)} %copy-done.2, pred[]{:T(512)S(6)} %eq.251, f32[2,4096,256]{2,1,0:T(8,128)} %mul.143), kind=kLoop, calls=%fused_computation.1 | loop fusion | flops 14680064 | bytes 37748736 | tf_op jit(solution)/shard_map/convert_element_type | solution.py:25
  420.5 75.5 %all-to-all-start = ((bf16[4,64,2,4096]{3,2,0,1:T(2,128)(2,1)}), bf16[4,64,2,4096]{3,2,0,1:T(2,128)(2,1)}, u32[]{:S(2)}, u32[]{:S(2)}) async-start(bf16[4,64,2,4096]{3,2,0,1:T(2,128)(2,1)} %copy.39), calls=%async_computation | async-start | bytes 8388608 | tf_op jit(solution)/shard_map/all_to_all | solution.py:96
  496.0 9.7 %copy.45 = bf16[4,64,2,4096]{3,2,1,0:T(2,128)(2,1)} copy(bf16[4,64,2,4096]{3,2,0,1:T(2,128)(2,1)} %all-to-all-done.2) | data formatting | bytes 8388608 | tf_op jit(solution)/shard_map/all_to_all | solution.py:96
  519.8 11.9 %convolution_convert_fusion = bf16[512,4096]{1,0:T(8,128)(2,1)} fusion(f32[32,8,32,128]{3,2,1,0:T(8,128)} %bitcast.101, bf16[1,256,4096]{2,1,0:T(8,128)(2,1)} %broadcast_select_fusion.1, f32[512,256]{1,0:T(8,128)S(1)} %fusion.6, bf16[512,4096]{1,0:T(8,128)(2,1)} %reshape.190, bf16[2,4096,256]{2,1,0:T(8,128)(2,1)} %get-tuple-element.6), kind=kOutput, calls=%fused_computation.4 | convolution fusion | flops 2153512960 | bytes 17301504 | tf_op jit(solution)/shard_map/dot_general | solution.py:43
  531.7 7.6 %convert_element_type.200 = bf16[4,64,2,4096]{3,2,1,0:T(2,128)(2,1)} reshape(bf16[512,4096]{1,0:T(8,128)(2,1)} %convolution_convert_fusion) | data formatting | bytes 8388608 | tf_op jit(solution)/shard_map/convert_element_type | solution.py:67
  546.5 44.4 %all-to-all-done = bf16[4,64,2,4096]{3,2,0,1:T(2,128)(2,1)} async-done(((bf16[4,64,2,4096]{3,2,0,1:T(2,128)(2,1)}), bf16[4,64,2,4096]{3,2,0,1:T(2,128)(2,1)}, u32[]{:S(2)}, u32[]{:S(2)}) %all-to-all-start) | async-done | bytes 4194336 | tf_op jit(solution)/shard_map/all_to_all | solution.py:96
  590.9 9.7 %copy.40 = bf16[4,64,2,4096]{3,2,1,0:T(2,128)(2,1)} copy(bf16[4,64,2,4096]{3,2,0,1:T(2,128)(2,1)} %all-to-all-done) | data formatting | bytes 8388608 | tf_op jit(solution)/shard_map/all_to_all | solution.py:96
  614.7 11.4 %convolution_convert_fusion.2 = bf16[512,4096]{1,0:T(8,128)(2,1)} fusion(f32[32,8,32,128]{3,2,1,0:T(8,128)} %bitcast.102, bf16[1,256,4096]{2,1,0:T(8,128)(2,1)S(1)} %copy-done.1, bf16[512,4096]{1,0:T(8,128)(2,1)} %reshape.186, bf16[2,4096,256]{2,1,0:T(8,128)(2,1)} %get-tuple-element.12, f32[512,256]{1,0:T(8,128)S(1)} %fusion.9), kind=kOutput, calls=%fused_computation.6 | convolution fusion | flops 2153512960 | bytes 17301504 | tf_op jit(solution)/shard_map/dot_general | solution.py:43
  626.1 7.7 %convert_element_type.179 = bf16[4,64,2,4096]{3,2,1,0:T(2,128)(2,1)} reshape(bf16[512,4096]{1,0:T(8,128)(2,1)} %convolution_convert_fusion.2) | data formatting | bytes 8388608 | tf_op jit(solution)/shard_map/convert_element_type | solution.py:67
  651.3 35.9 %reduce-scatter.3.cloned.1.call-done = bf16[1,64,2,4096]{3,1,2,0:T(8,128)(2,1)} async-done(((bf16[4,64,2,4096]{3,1,2,0:T(8,128)(2,1)}), bf16[1,64,2,4096]{3,1,2,0:T(8,128)(2,1)}) %reduce-scatter.3.cloned.1.call-update) | async-done | bytes 1048592 | tf_op jit(solution)/shard_map/reduce_scatter | solution.py:66
  690.5 10.8 %all-to-all-start.1 = ((bf16[1,64,2,4096]{3,2,0,1:T(2,128)(2,1)}), bf16[1,64,2,4096]{3,2,0,1:T(2,128)(2,1)S(1)}, u32[]{:S(2)}, u32[]{:S(2)}) async-start(bf16[1,64,2,4096]{3,2,0,1:T(2,128)(2,1)} %copy.43), calls=%async_computation.2 | async-start | bytes 2097152 | tf_op jit(solution)/shard_map/all_to_all | solution.py:69
  704.9 24.4 %all-to-all-done.1 = bf16[1,64,2,4096]{3,2,0,1:T(2,128)(2,1)S(1)} async-done(((bf16[1,64,2,4096]{3,2,0,1:T(2,128)(2,1)}), bf16[1,64,2,4096]{3,2,0,1:T(2,128)(2,1)S(1)}, u32[]{:S(2)}, u32[]{:S(2)}) %all-to-all-start.1) | async-done | bytes 1048608 | tf_op jit(solution)/shard_map/all_to_all | solution.py:69
  (97 shorter events, 102.0 us)
Async XLA Ops:
  7.2 695.7 %copy-start = (f32[8,8]{1,0:T(8,128)S(1)}, f32[8,8]{1,0:T(8,128)}, u32[]{:S(2)}) copy-start(f32[8,8]{1,0:T(8,128)} %param.18) | copy-start | bytes 772
  54.1 23.9 %copy-start.1 = (bf16[1,256,4096]{2,1,0:T(8,128)(2,1)S(1)}, bf16[1,256,4096]{2,1,0:T(8,128)(2,1)}, u32[]{:S(2)}) copy-start(bf16[1,256,4096]{2,1,0:T(8,128)(2,1)} %param.24) | copy-start | bytes 6291460
  54.1 24.0 %copy-start.6 = (bf16[1,2,32,2]{2,3,1,0:T(2,128)(2,1)S(1)}, bf16[1,2,32,2]{2,3,1,0:T(2,128)(2,1)}, u32[]{:S(2)}) copy-start(bf16[1,2,32,2]{2,3,1,0:T(2,128)(2,1)} %param.23) | copy-start | bytes 772
  54.1 29.3 %copy-start.7 = (bf16[1,2,32]{2,1,0:T(2,128)(2,1)S(1)}, bf16[1,2,32]{2,1,0:T(2,128)(2,1)}, u32[]{:S(2)}) copy-start(bf16[1,2,32]{2,1,0:T(2,128)(2,1)} %param.25) | copy-start | bytes 388
  54.1 29.4 %copy-start.4 = (s32[8,8]{1,0:T(8,128)S(1)}, s32[8,8]{1,0:T(8,128)}, u32[]{:S(2)}) copy-start(s32[8,8]{1,0:T(8,128)} %param.15) | copy-start | bytes 772
  54.1 39.5 %copy-start.5 = (s32[64]{0:T(128)S(1)}, s32[64]{0:T(128)}, u32[]{:S(2)}) copy-start(s32[64]{0:T(128)} %param.20) | copy-start | bytes 772
  54.1 366.4 %all-to-all-start.2 = ((bf16[4,64,2,4096]{3,2,0,1:T(2,128)(2,1)}), bf16[4,64,2,4096]{3,2,0,1:T(2,128)(2,1)}, u32[]{:S(2)}, u32[]{:S(2)}) async-start(bf16[4,64,2,4096]{3,2,0,1:T(2,128)(2,1)} %copy.44), calls=%async_computation.3 | async-start | bytes 8388608 | tf_op jit(solution)/shard_map/all_to_all | solution.py:96
  72.6 336.1 %collective-permute-start = (bf16[1,2,4096,256]{3,2,1,0:T(8,128)(2,1)}, bf16[1,2,4096,256]{3,2,1,0:T(8,128)(2,1)}, u32[]{:S(2)}, u32[]{:S(2)}) collective-permute-start(bf16[1,2,4096,256]{3,2,1,0:T(8,128)(2,1)} %param.22), channel_id=1, source_target_pairs={{0,128},{128,0},{4,132},{132,4},{8,136},{136,8},{12,140},{140,12},... | collective-permute-start | bytes 12582920 | tf_op jit(solution)/shard_map/ppermute | solution.py:14
  78.0 329.0 %collective-permute-start.2 = (bf16[1,256,4096]{2,1,0:T(8,128)(2,1)S(1)}, bf16[1,256,4096]{2,1,0:T(8,128)(2,1)}, u32[]{:S(2)}, u32[]{:S(2)}) collective-permute-start(bf16[1,256,4096]{2,1,0:T(8,128)(2,1)S(1)} %copy-done.1), channel_id=1, source_target_pairs={{0,128},{128,0},{4,132},{132,4},{8,136},{136,8},{12,140},{140,12},... | collective-permute-start | bytes 6291464 | tf_op jit(solution)/shard_map/ppermute | solution.py:14
  78.2 294.2 %collective-permute-start.1 = (bf16[1,2,32,2]{2,3,1,0:T(2,128)(2,1)S(1)}, bf16[1,2,32,2]{2,3,1,0:T(2,128)(2,1)S(1)}, u32[]{:S(2)}, u32[]{:S(2)}) collective-permute-start(bf16[1,2,32,2]{2,3,1,0:T(2,128)(2,1)S(1)} %copy-done.6), channel_id=1, source_target_pairs={{0,128},{128,0},{4,132},{132,4},{8,136},{136,8},{12,140},{140,12},... | collective-permute-start | bytes 776 | tf_op jit(solution)/shard_map/ppermute | solution.py:14
  83.4 288.4 %collective-permute-start.3 = (bf16[1,2,32]{2,1,0:T(2,128)(2,1)S(1)}, bf16[1,2,32]{2,1,0:T(2,128)(2,1)S(1)}, u32[]{:S(2)}, u32[]{:S(2)}) collective-permute-start(bf16[1,2,32]{2,1,0:T(2,128)(2,1)S(1)} %copy-done.7), channel_id=1, source_target_pairs={{0,128},{128,0},{4,132},{132,4},{8,136},{136,8},{12,140},{140,12},... | collective-permute-start | bytes 392 | tf_op jit(solution)/shard_map/ppermute | solution.py:14
  116.8 10.2 %copy-start.9 = (s32[64]{0:T(128)S(1)}, s32[64]{0:T(128)}, u32[]{:S(2)}) copy-start(s32[64]{0:T(128)} %param.21) | copy-start | bytes 772
  407.0 2.9 copy-start.2
  420.5 170.4 %all-to-all-start = ((bf16[4,64,2,4096]{3,2,0,1:T(2,128)(2,1)}), bf16[4,64,2,4096]{3,2,0,1:T(2,128)(2,1)}, u32[]{:S(2)}, u32[]{:S(2)}) async-start(bf16[4,64,2,4096]{3,2,0,1:T(2,128)(2,1)} %copy.39), calls=%async_computation | async-start | bytes 8388608 | tf_op jit(solution)/shard_map/all_to_all | solution.py:96
  496.0 144.9 %reduce-scatter.5.cloned.1.call-start = ((), (), s32[]{:S(2)}) async-start(), calls=%async_computation.7 | async-start | bytes 5242880 | tf_op jit(solution)/shard_map/reduce_scatter | solution.py:66
  546.4 140.7 %reduce-scatter.3.cloned.1.call-start = ((), (), s32[]{:S(2)}) async-start(), calls=%async_computation.6 | async-start | bytes 5242880 | tf_op jit(solution)/shard_map/reduce_scatter | solution.py:66
  640.8 60.4 %copy-start.3 = (s32[8,8]{1,0:T(8,128)S(1)}, s32[8,8]{1,0:T(8,128)}, u32[]{:S(2)}) copy-start(s32[8,8]{1,0:T(8,128)} %param.16) | copy-start | bytes 772
  640.8 62.3 %copy-start.8 = (f32[8,8]{1,0:T(8,128)S(1)}, f32[8,8]{1,0:T(8,128)}, u32[]{:S(2)}) copy-start(f32[8,8]{1,0:T(8,128)} %param.17) | copy-start | bytes 772
  644.2 46.3 %all-to-all-start.3 = ((bf16[1,64,2,4096]{3,2,0,1:T(2,128)(2,1)}), bf16[1,64,2,4096]{3,2,0,1:T(2,128)(2,1)S(1)}, u32[]{:S(2)}, u32[]{:S(2)}) async-start(bf16[1,64,2,4096]{3,2,0,1:T(2,128)(2,1)} %copy.48), calls=%async_computation.5 | async-start | bytes 2097152 | tf_op jit(solution)/shard_map/all_to_all | solution.py:69
  690.5 38.9 %all-to-all-start.1 = ((bf16[1,64,2,4096]{3,2,0,1:T(2,128)(2,1)}), bf16[1,64,2,4096]{3,2,0,1:T(2,128)(2,1)S(1)}, u32[]{:S(2)}, u32[]{:S(2)}) async-start(bf16[1,64,2,4096]{3,2,0,1:T(2,128)(2,1)} %copy.43), calls=%async_computation.2 | async-start | bytes 2097152 | tf_op jit(solution)/shard_map/all_to_all | solution.py:69
Sparse Core Ops, SparseCore 0:
  546.6 49.7 reduce-scatter.4
  640.9 46.1 reduce-scatter.2
where the time goes:
time: 749 us; the launch traced here: 738 us
  waiting for transfers between devices  348 us (46%)
  local copies, waits for them, and re-layouts  148 us (20%)
  starting transfers between devices  123 us (16%)
  matrix products  40.9 us (5%)
  blocking collectives  40.4 us (5%)
  other arithmetic  22.3 us (3%)
  between operations  15.4 us (2%)
    ppermute x4, waiting for transfers between devices, partner(): return lax.ppermute(block, axis, route)  244 us
    all_to_all x2, starting transfers between devices, decode_step(): lax.all_to_all(outgoing, 'expert', split_axis=1, concat_axis=1, tiled=True)  93.9 us
    all_to_all x2, waiting for transfers between devices, decode_step(): lax.all_to_all(outgoing, 'expert', split_axis=1, concat_axis=1, tiled=True)  44.4 us
    mul x6, local copies, waits for them, and re-layouts, dequantize(): scaled = blocked * scales.astype(jnp.float32)[..., :, None, :, None]  39 us
    reduce_scatter x2, waiting for transfers between devices, finish(): lax.psum_scatter(partial_terms.astype(jnp.bfloat16), 'replica', scatter_d...  35.9 us
    reshape x4, local copies, waits for them, and re-layouts, decode_step(): outgoing.astype(jnp.bfloat16).reshape(copies, experts, capacity, features)  35.8 us
    convert_element_type x4, local copies, waits for them, and re-layouts, finish(): partial_terms.astype(jnp.bfloat16)  29.4 us
    all_to_all x2, waiting for transfers between devices, finish(): lax.all_to_all(summed, 'expert', split_axis=1, concat_axis=1, tiled=True)  24.4 us
  transfers between devices with their start and end apart: 10, of which 4 were waited for; matrix products, arithmetic and copies ran while one was open for 25% of the time, Pallas kernels for 0%

commit v1 on v0

--- a/solution.py
+++ b/solution.py
@@ -78,7 +78,15 @@
     normed = rms_normed(hidden, norm_gain)
     own_picks = pick_slots(routes, owner_slots, experts, capacity)
     pooled, pooled_routes = (
-        lax.all_gather(normed, "replica", axis=0, tiled=True),
+        jnp.concatenate(
+            lax.all_to_all(
+                jnp.stack(lax.axis_size("replica") * [normed], axis=0),
+                axis_name="replica",
+                split_axis=0,
+                concat_axis=0,
+            ),
+            axis=0,
+        ),
         lax.all_gather(routes, "replica", axis=0, tiled=True),
     )
     grouped = pooled_routes.reshape(copies, tokens_here, top_count)

time: 749 us -> 777 us (1.037)
  waiting for transfers between devices: 348 us -> 380 us
  blocking collectives: 40.4 us -> 20.9 us
  other arithmetic: 22.3 us -> 32.2 us
    ppermute x4, waiting for transfers between devices: 244 us -> 275 us  [partner(): return lax.ppermute(block, axis, route)]
    all_gather x2 -> x0, blocking collectives: 19.9 us -> none  [decode_step(): lax.all_gather(normed, 'replica', axis=0, tiled=True)]
    convert_element_type x1, other arithmetic: 10.6 us -> 20.4 us  [dequantize(): return scaled.reshape(values.shape).astype(jnp.bfloat16)]
    all_to_all x0 -> x2, starting transfers between devices: none -> 8.24 us  [decode_step(): lax.all_to_all(jnp.stack(lax.axis_size('replica') * [normed], axis=0), ax...]
  transfers between devices with their start and end apart: 10 -> 12, of which waited for: 4 -> 4; matrix products, arithmetic and copies ran while one was open for 25% -> 28% of each run, Pallas kernels for 0% -> 0%
where the time goes in v1:
time: 777 us; the launch traced here: 768 us
  waiting for transfers between devices  380 us (49%)
  local copies, waits for them, and re-layouts  149 us (19%)
  starting transfers between devices  129 us (17%)
  matrix products  40.9 us (5%)
  other arithmetic  32.2 us (4%)
  blocking collectives  20.9 us (3%)
  between operations  15.4 us (2%)
    ppermute x4, waiting for transfers between devices, partner(): return lax.ppermute(block, axis, route)  275 us
    all_to_all x2, starting transfers between devices, decode_step(): lax.all_to_all(outgoing, 'expert', split_axis=1, concat_axis=1, tiled=True)  91.5 us
    all_to_all x2, waiting for transfers between devices, decode_step(): lax.all_to_all(outgoing, 'expert', split_axis=1, concat_axis=1, tiled=True)  44.4 us
    mul x6, local copies, waits for them, and re-layouts, dequantize(): scaled = blocked * scales.astype(jnp.float32)[..., :, None, :, None]  39 us
    reduce_scatter x2, waiting for transfers between devices, finish(): lax.psum_scatter(partial_terms.astype(jnp.bfloat16), 'replica', scatter_d...  36.9 us
    reshape x4, local copies, waits for them, and re-layouts, decode_step(): outgoing.astype(jnp.bfloat16).reshape(copies, experts, capacity, features)  35.5 us
    convert_element_type x4, local copies, waits for them, and re-layouts, finish(): partial_terms.astype(jnp.bfloat16)  29.4 us
    all_to_all x2, waiting for transfers between devices, finish(): lax.all_to_all(summed, 'expert', split_axis=1, concat_axis=1, tiled=True)  24.4 us
  transfers between devices with their start and end apart: 12, of which 4 were waited for; matrix products, arithmetic and copies ran while one was open for 28% of the time, Pallas kernels for 0%

profile of v1, /device:TPU:1, one launch (start us, length us, event | category | flops | bytes accessed | tf_op | source)
XLA Modules:
  0.0 767.7 jit_solution(16300633110477485671)
XLA Ops:
  17.2 10.1 %all_gather.7 = s32[32,8]{1,0:T(8,128)S(1)} all-gather(s32[8,8]{1,0:T(8,128)} %param.16), channel_id=1, replica_groups=mesh['expert'=64,'replica'=4] {'replica'}, dimensions={0}, use_global_device_ids=true | all-gather | bytes 1280 | tf_op jit(solution)/shard_map/all_gather | solution.py:90
  36.2 7.6 reshape.185
  43.8 10.1 %copy.44 = bf16[4,64,2,4096]{3,2,0,1:T(2,128)(2,1)} copy(bf16[4,64,2,4096]{3,2,1,0:T(2,128)(2,1)} %reshape.185) | data formatting | bytes 8388608 | tf_op jit(solution)/shard_map/reshape | solution.py:103
  54.0 16.1 %all-to-all-start.4 = ((bf16[4,64,2,4096]{3,2,0,1:T(2,128)(2,1)}), bf16[4,64,2,4096]{3,2,0,1:T(2,128)(2,1)}, u32[]{:S(2)}, u32[]{:S(2)}) async-start(bf16[4,64,2,4096]{3,2,0,1:T(2,128)(2,1)} %copy.44), calls=%async_computation.5 | async-start | bytes 8388608 | tf_op jit(solution)/shard_map/all_to_all | solution.py:104
  81.1 10.9 %all_gather.6 = s32[32,8]{1,0:T(8,128)S(1)} all-gather(s32[8,8]{1,0:T(8,128)S(1)} %copy-done.4), channel_id=1, replica_groups=mesh['expert'=64,'replica'=4] {'replica'}, dimensions={0}, use_global_device_ids=true | all-gather | bytes 1280 | tf_op jit(solution)/shard_map/all_gather | solution.py:90
  94.7 274.7 %collective-permute-done.3 = bf16[1,2,32]{2,1,0:T(2,128)(2,1)S(1)} collective-permute-done((bf16[1,2,32]{2,1,0:T(2,128)(2,1)S(1)}, bf16[1,2,32]{2,1,0:T(2,128)(2,1)S(1)}, u32[]{:S(2)}, u32[]{:S(2)}) %collective-permute-start.3) | collective-permute-done | bytes 160 | tf_op jit(solution)/shard_map/ppermute | solution.py:14
  376.0 11.5 %mul.143 = f32[2,4096,256]{2,1,0:T(8,128)} reshape(f32[2,32,128,2,128]{4,3,2,1,0:T(2,128)} %mul.142) | data formatting | bytes 16777216 | tf_op jit(solution)/shard_map/mul | solution.py:24
  393.0 11.5 %mul.159 = f32[2,4096,256]{2,1,0:T(8,128)} reshape(f32[2,32,128,2,128]{4,3,2,1,0:T(2,128)} %mul.158) | data formatting | bytes 16777216 | tf_op jit(solution)/shard_map/mul | solution.py:24
  407.9 7.6 reshape.182
  415.5 10.2 %copy.39 = bf16[4,64,2,4096]{3,2,0,1:T(2,128)(2,1)} copy(bf16[4,64,2,4096]{3,2,1,0:T(2,128)(2,1)} %reshape.182) | data formatting | bytes 8388608 | tf_op jit(solution)/shard_map/reshape | solution.py:103
  428.6 20.4 %fusion = (bf16[2,4096,256]{2,1,0:T(8,128)(2,1)}, bf16[1,2,4096,256]{3,2,1,0:T(8,128)(2,1)}, bf16[2,4096,256]{2,1,0:T(8,128)(2,1)}) fusion(f32[2,4096,256]{2,1,0:T(8,128)} %mul.159, bf16[1,2,4096,256]{3,2,1,0:T(8,128)(2,1)} %collective-permute-done, bf16[1,2,4096,256]{3,2,1,0:T(8,128)(2,1)S(1)} %copy-done.2, pred[]{:T(512)S(6)} %eq.251, f32[2,4096,256]{2,1,0:T(8,128)} %mul.143), kind=kLoop, calls=%fused_computation.1 | loop fusion | flops 14680064 | bytes 37748736 | tf_op jit(solution)/shard_map/convert_element_type | solution.py:25
  449.0 75.4 %all-to-all-start.1 = ((bf16[4,64,2,4096]{3,2,0,1:T(2,128)(2,1)}), bf16[4,64,2,4096]{3,2,0,1:T(2,128)(2,1)}, u32[]{:S(2)}, u32[]{:S(2)}) async-start(bf16[4,64,2,4096]{3,2,0,1:T(2,128)(2,1)} %copy.39), calls=%async_computation.1 | async-start | bytes 8388608 | tf_op jit(solution)/shard_map/all_to_all | solution.py:104
  524.5 9.7 %copy.45 = bf16[4,64,2,4096]{3,2,1,0:T(2,128)(2,1)} copy(bf16[4,64,2,4096]{3,2,0,1:T(2,128)(2,1)} %all-to-all-done.4) | data formatting | bytes 8388608 | tf_op jit(solution)/shard_map/all_to_all | solution.py:104
  534.2 7.2 reshape.186
  548.1 11.9 %convolution_convert_fusion = bf16[512,4096]{1,0:T(8,128)(2,1)} fusion(f32[32,8,32,128]{3,2,1,0:T(8,128)} %bitcast.97, bf16[1,256,4096]{2,1,0:T(8,128)(2,1)} %broadcast_select_fusion.1, f32[512,256]{1,0:T(8,128)S(1)} %fusion.6, bf16[512,4096]{1,0:T(8,128)(2,1)} %reshape.186, bf16[2,4096,256]{2,1,0:T(8,128)(2,1)} %get-tuple-element.6), kind=kOutput, calls=%fused_computation.4 | convolution fusion | flops 2153512960 | bytes 17301504 | tf_op jit(solution)/shard_map/dot_general | solution.py:43
  560.0 7.6 convert_element_type.200
  575.0 44.3 %all-to-all-done.1 = bf16[4,64,2,4096]{3,2,0,1:T(2,128)(2,1)} async-done(((bf16[4,64,2,4096]{3,2,0,1:T(2,128)(2,1)}), bf16[4,64,2,4096]{3,2,0,1:T(2,128)(2,1)}, u32[]{:S(2)}, u32[]{:S(2)}) %all-to-all-start.1) | async-done | bytes 4194336 | tf_op jit(solution)/shard_map/all_to_all | solution.py:104
  619.4 9.8 %copy.40 = bf16[4,64,2,4096]{3,2,1,0:T(2,128)(2,1)} copy(bf16[4,64,2,4096]{3,2,0,1:T(2,128)(2,1)} %all-to-all-done.1) | data formatting | bytes 8388608 | tf_op jit(solution)/shard_map/all_to_all | solution.py:104
  629.2 7.2 reshape.183
  643.0 11.4 %convolution_convert_fusion.2 = bf16[512,4096]{1,0:T(8,128)(2,1)} fusion(f32[32,8,32,128]{3,2,1,0:T(8,128)} %bitcast.98, bf16[1,256,4096]{2,1,0:T(8,128)(2,1)S(1)} %copy-done.1, bf16[512,4096]{1,0:T(8,128)(2,1)} %reshape.183, bf16[2,4096,256]{2,1,0:T(8,128)(2,1)} %get-tuple-element.12, f32[512,256]{1,0:T(8,128)S(1)} %fusion.9), kind=kOutput, calls=%fused_computation.6 | convolution fusion | flops 2153512960 | bytes 17301504 | tf_op jit(solution)/shard_map/dot_general | solution.py:43
  654.4 7.6 convert_element_type.179
  679.6 36.9 %reduce-scatter.3.cloned.1.call-done = bf16[1,64,2,4096]{3,1,2,0:T(8,128)(2,1)} async-done(((bf16[4,64,2,4096]{3,1,2,0:T(8,128)(2,1)}), bf16[1,64,2,4096]{3,1,2,0:T(8,128)(2,1)}) %reduce-scatter.3.cloned.1.call-update) | async-done | bytes 1048592 | tf_op jit(solution)/shard_map/reduce_scatter | solution.py:66
  719.9 10.7 %all-to-all-start.2 = ((bf16[1,64,2,4096]{3,2,0,1:T(2,128)(2,1)}), bf16[1,64,2,4096]{3,2,0,1:T(2,128)(2,1)S(1)}, u32[]{:S(2)}, u32[]{:S(2)}) async-start(bf16[1,64,2,4096]{3,2,0,1:T(2,128)(2,1)} %copy.43), calls=%async_computation.3 | async-start | bytes 2097152 | tf_op jit(solution)/shard_map/all_to_all | solution.py:69
  734.4 24.4 %all-to-all-done.2 = bf16[1,64,2,4096]{3,2,0,1:T(2,128)(2,1)S(1)} async-done(((bf16[1,64,2,4096]{3,2,0,1:T(2,128)(2,1)}), bf16[1,64,2,4096]{3,2,0,1:T(2,128)(2,1)S(1)}, u32[]{:S(2)}, u32[]{:S(2)}) %all-to-all-start.2) | async-done | bytes 1048608 | tf_op jit(solution)/shard_map/all_to_all | solution.py:69
  (101 shorter events, 97.2 us)
Async XLA Ops:
  7.2 725.1 %copy-start = (f32[8,8]{1,0:T(8,128)S(1)}, f32[8,8]{1,0:T(8,128)}, u32[]{:S(2)}) copy-start(f32[8,8]{1,0:T(8,128)} %param.18) | copy-start | bytes 772
  10.9 17.9 %all-to-all-start.3 = ((bf16[4,8,4096]{2,1,0:T(8,128)(2,1)}), bf16[4,8,4096]{2,1,0:T(8,128)(2,1)S(1)}, u32[]{:S(2)}, u32[]{:S(2)}) async-start(bf16[4,8,4096]{2,1,0:T(8,128)(2,1)} %stack.5), calls=%async_computation.4 | async-start | bytes 524288 | tf_op jit(solution)/shard_map/all_to_all | solution.py:82
  29.5 24.5 %all-to-all-start = ((bf16[4,8,4096]{2,1,0:T(8,128)(2,1)}), bf16[4,8,4096]{2,1,0:T(8,128)(2,1)S(1)}, u32[]{:S(2)}, u32[]{:S(2)}) async-start(bf16[4,8,4096]{2,1,0:T(8,128)(2,1)} %stack.4), calls=%async_computation | async-start | bytes 524288 | tf_op jit(solution)/shard_map/all_to_all | solution.py:82
  54.0 21.6 %copy-start.1 = (bf16[1,256,4096]{2,1,0:T(8,128)(2,1)S(1)}, bf16[1,256,4096]{2,1,0:T(8,128)(2,1)}, u32[]{:S(2)}) copy-start(bf16[1,256,4096]{2,1,0:T(8,128)(2,1)} %param.24) | copy-start | bytes 6291460
  54.0 21.7 %copy-start.6 = (bf16[1,2,32,2]{2,3,1,0:T(2,128)(2,1)S(1)}, bf16[1,2,32,2]{2,3,1,0:T(2,128)(2,1)}, u32[]{:S(2)}) copy-start(bf16[1,2,32,2]{2,3,1,0:T(2,128)(2,1)} %param.23) | copy-start | bytes 772
  54.0 27.0 %copy-start.7 = (bf16[1,2,32]{2,1,0:T(2,128)(2,1)S(1)}, bf16[1,2,32]{2,1,0:T(2,128)(2,1)}, u32[]{:S(2)}) copy-start(bf16[1,2,32]{2,1,0:T(2,128)(2,1)} %param.25) | copy-start | bytes 388
  54.0 27.1 %copy-start.4 = (s32[8,8]{1,0:T(8,128)S(1)}, s32[8,8]{1,0:T(8,128)}, u32[]{:S(2)}) copy-start(s32[8,8]{1,0:T(8,128)} %param.15) | copy-start | bytes 772
  54.0 38.0 %copy-start.5 = (s32[64]{0:T(128)S(1)}, s32[64]{0:T(128)}, u32[]{:S(2)}) copy-start(s32[64]{0:T(128)} %param.20) | copy-start | bytes 772
  54.0 39.3 %copy-start.9 = (s32[64]{0:T(128)S(1)}, s32[64]{0:T(128)}, u32[]{:S(2)}) copy-start(s32[64]{0:T(128)} %param.21) | copy-start | bytes 772
  54.0 395.0 %all-to-all-start.4 = ((bf16[4,64,2,4096]{3,2,0,1:T(2,128)(2,1)}), bf16[4,64,2,4096]{3,2,0,1:T(2,128)(2,1)}, u32[]{:S(2)}, u32[]{:S(2)}) async-start(bf16[4,64,2,4096]{3,2,0,1:T(2,128)(2,1)} %copy.44), calls=%async_computation.5 | async-start | bytes 8388608 | tf_op jit(solution)/shard_map/all_to_all | solution.py:104
  70.1 357.2 %collective-permute-start = (bf16[1,2,4096,256]{3,2,1,0:T(8,128)(2,1)}, bf16[1,2,4096,256]{3,2,1,0:T(8,128)(2,1)}, u32[]{:S(2)}, u32[]{:S(2)}) collective-permute-start(bf16[1,2,4096,256]{3,2,1,0:T(8,128)(2,1)} %param.22), channel_id=1, source_target_pairs={{0,128},{128,0},{4,132},{132,4},{8,136},{136,8},{12,140},{140,12},... | collective-permute-start | bytes 12582920 | tf_op jit(solution)/shard_map/ppermute | solution.py:14
  75.6 350.0 %collective-permute-start.2 = (bf16[1,256,4096]{2,1,0:T(8,128)(2,1)S(1)}, bf16[1,256,4096]{2,1,0:T(8,128)(2,1)}, u32[]{:S(2)}, u32[]{:S(2)}) collective-permute-start(bf16[1,256,4096]{2,1,0:T(8,128)(2,1)S(1)} %copy-done.1), channel_id=1, source_target_pairs={{0,128},{128,0},{4,132},{132,4},{8,136},{136,8},{12,140},{140,12},... | collective-permute-start | bytes 6291464 | tf_op jit(solution)/shard_map/ppermute | solution.py:14
  75.7 294.2 %collective-permute-start.1 = (bf16[1,2,32,2]{2,3,1,0:T(2,128)(2,1)S(1)}, bf16[1,2,32,2]{2,3,1,0:T(2,128)(2,1)S(1)}, u32[]{:S(2)}, u32[]{:S(2)}) collective-permute-start(bf16[1,2,32,2]{2,3,1,0:T(2,128)(2,1)S(1)} %copy-done.6), channel_id=1, source_target_pairs={{0,128},{128,0},{4,132},{132,4},{8,136},{136,8},{12,140},{140,12},... | collective-permute-start | bytes 776 | tf_op jit(solution)/shard_map/ppermute | solution.py:14
  81.0 288.4 %collective-permute-start.3 = (bf16[1,2,32]{2,1,0:T(2,128)(2,1)S(1)}, bf16[1,2,32]{2,1,0:T(2,128)(2,1)S(1)}, u32[]{:S(2)}, u32[]{:S(2)}) collective-permute-start(bf16[1,2,32]{2,1,0:T(2,128)(2,1)S(1)} %copy-done.7), channel_id=1, source_target_pairs={{0,128},{128,0},{4,132},{132,4},{8,136},{136,8},{12,140},{140,12},... | collective-permute-start | bytes 392 | tf_op jit(solution)/shard_map/ppermute | solution.py:14
  425.6 2.9 copy-start.2
  449.0 170.3 %all-to-all-start.1 = ((bf16[4,64,2,4096]{3,2,0,1:T(2,128)(2,1)}), bf16[4,64,2,4096]{3,2,0,1:T(2,128)(2,1)}, u32[]{:S(2)}, u32[]{:S(2)}) async-start(bf16[4,64,2,4096]{3,2,0,1:T(2,128)(2,1)} %copy.39), calls=%async_computation.1 | async-start | bytes 8388608 | tf_op jit(solution)/shard_map/all_to_all | solution.py:104
  524.5 144.8 %reduce-scatter.5.cloned.1.call-start = ((), (), s32[]{:S(2)}) async-start(), calls=%async_computation.9 | async-start | bytes 5242880 | tf_op jit(solution)/shard_map/reduce_scatter | solution.py:66
  574.7 141.8 %reduce-scatter.3.cloned.1.call-start = ((), (), s32[]{:S(2)}) async-start(), calls=%async_computation.8 | async-start | bytes 5242880 | tf_op jit(solution)/shard_map/reduce_scatter | solution.py:66
  669.2 61.5 %copy-start.3 = (s32[8,8]{1,0:T(8,128)S(1)}, s32[8,8]{1,0:T(8,128)}, u32[]{:S(2)}) copy-start(s32[8,8]{1,0:T(8,128)} %param.16) | copy-start | bytes 772
  669.2 63.3 %copy-start.8 = (f32[8,8]{1,0:T(8,128)S(1)}, f32[8,8]{1,0:T(8,128)}, u32[]{:S(2)}) copy-start(f32[8,8]{1,0:T(8,128)} %param.17) | copy-start | bytes 772
  672.5 47.4 %all-to-all-start.5 = ((bf16[1,64,2,4096]{3,2,0,1:T(2,128)(2,1)}), bf16[1,64,2,4096]{3,2,0,1:T(2,128)(2,1)S(1)}, u32[]{:S(2)}, u32[]{:S(2)}) async-start(bf16[1,64,2,4096]{3,2,0,1:T(2,128)(2,1)} %copy.48), calls=%async_computation.7 | async-start | bytes 2097152 | tf_op jit(solution)/shard_map/all_to_all | solution.py:69
  719.9 38.9 %all-to-all-start.2 = ((bf16[1,64,2,4096]{3,2,0,1:T(2,128)(2,1)}), bf16[1,64,2,4096]{3,2,0,1:T(2,128)(2,1)S(1)}, u32[]{:S(2)}, u32[]{:S(2)}) async-start(bf16[1,64,2,4096]{3,2,0,1:T(2,128)(2,1)} %copy.43), calls=%async_computation.3 | async-start | bytes 2097152 | tf_op jit(solution)/shard_map/all_to_all | solution.py:69
Sparse Core Ops, SparseCore 0:
  574.9 50.8 reduce-scatter.4
  669.3 47.1 reduce-scatter.2
